TPU v7x, 128 devices: a whole 4x4x4 slice. The times are simulated.
128 devices in a mesh: tm: 16 (over y, x), tile: 8 (over z, core).
Axes of the slice: x: 4, y: 4, z: 4, core: 2. Of those that a mesh axis runs over, the one named last changes fastest.
Arguments:
- queries: bfloat16 [16384, 1536], P(('tm', 'tile')), may hold values from -16 to 16
- keys: bfloat16 [16384, 1536], P(('tm', 'tile')), may hold values from -16 to 16
- values: bfloat16 [16384, 1536], P(('tm', 'tile')), may hold values from -6 to 6
- grad_out: bfloat16 [16384, 1536], P(('tm', 'tile')), may hold values from -6 to 6
- span_of_group: int32 [16], replicated, may hold values from 0 to 15, each once
- noise_level: int32 [16], replicated, may hold values from 0 to 999
- next_live: int32 [128], replicated, may hold values 0 or 1
- level_bias: float32 [1000, 12], replicated, may hold values from -2 to 2
Outputs:
- attended: bfloat16 [16384, 1536], P(('tm', 'tile'))
- grad_queries: bfloat16 [16384, 1536], P(('tm', 'tile'))
- grad_keys: bfloat16 [16384, 1536], P(('tm', 'tile'))
- grad_values: bfloat16 [16384, 1536], P(('tm', 'tile'))
Inputs may be any that keep to these rules, and one draw needn't show every extreme that they name: span_of_group is a permutation of 0 to 15.
All inputs are finite; a program needn't handle non-finite values.
Results may differ from a plain program's by a relative error of at most 0.019.
Values may be sent and summed in bfloat16 or wider, within the bound.
A program may use at most 256 MiB of HBM per device.

v0:
```python
import math
import jax
import jax.numpy as jnp
from jax import lax
from jax.sharding import PartitionSpec as P


def shifted(value, axis, by):
    count = lax.axis_size(axis)
    return lax.ppermute(value, axis, [(i, (i + by) % count) for i in range(count)])


def pick_entry(table, index):
    spots = jnp.arange(table.shape[0], dtype=jnp.int32)
    return jnp.sum(jnp.where(spots == index, table, 0), axis=0)


def per_device(queries, keys, values, grad_out, span_of_group, noise_level, next_live, level_bias):
    tok_rows, model_width = queries.shape
    head_count = level_bias.shape[1]
    head_width = model_width // head_count
    inv_root = 1.0 / math.sqrt(head_width)
    groups = lax.axis_size("tm")
    tile_count = lax.axis_size("tile")
    my_group = lax.axis_index("tm")
    my_tile = lax.axis_index("tile")
    group_ids = jnp.arange(groups, dtype=jnp.int32)
    own_span = pick_entry(span_of_group, my_group)
    level_of = jnp.sum(
        jnp.where(span_of_group[:, None] == group_ids[None, :], noise_level[None, :], 0), axis=1
    )
    level_ids = jnp.arange(level_bias.shape[0], dtype=jnp.int32)
    level_table = (level_of[:, None] == level_ids[None, :]).astype(jnp.float32)
    group_bias = jnp.dot(
        level_table, level_bias, precision=lax.Precision.HIGHEST, preferred_element_type=jnp.float32
    )
    second_half = jnp.arange(2 * tok_rows, dtype=jnp.int32) >= tok_rows
    first_half = jnp.logical_not(second_half)
    live_table = next_live.reshape(groups, tile_count)
    live_here = pick_entry(next_live, my_group * tile_count + my_tile)
    attend = span_of_group <= own_span
    key_mask = attend[:, None] & (first_half[None, :] | (live_here == 1))
    near_k, near_v = shifted((keys, values), "tile", -1)
    past_k, past_v, ahead_k, ahead_v = (
        lax.all_gather(keys[None], "tm", axis=0, tiled=True),
        lax.all_gather(values[None], "tm", axis=0, tiled=True),
        lax.all_gather(near_k[None], "tm", axis=0, tiled=True),
        lax.all_gather(near_v[None], "tm", axis=0, tiled=True),
    )
    all_keys = jnp.concatenate([past_k, ahead_k], axis=1).reshape(
        groups, 2 * tok_rows, head_count, head_width
    )
    all_values = jnp.concatenate([past_v, ahead_v], axis=1).reshape(
        groups, 2 * tok_rows, head_count, head_width
    )
    query_heads = queries.reshape(tok_rows, head_count, head_width)
    grad_heads = grad_out.reshape(tok_rows, head_count, head_width)
    scores = jnp.einsum("qhe,jkhe->jhqk", query_heads, all_keys, preferred_element_type=jnp.float32)
    scores = scores * inv_root + group_bias[:, :, None, None]
    scores = jnp.where(key_mask[:, None, None, :], scores, -1e30)
    row_peak = jnp.max(scores, axis=(0, 3))
    log_total = row_peak + jnp.log(
        jnp.sum(jnp.exp(scores - row_peak[None, :, :, None]), axis=(0, 3))
    )
    weights_full = jnp.exp(scores - log_total[None, :, :, None])
    weights_low = weights_full.astype(jnp.bfloat16)
    attended = jnp.einsum(
        "jhqk,jkhe->qhe", weights_low, all_values, preferred_element_type=jnp.float32
    ).astype(jnp.bfloat16)
    row_delta = jnp.sum(grad_heads.astype(jnp.float32) * attended.astype(jnp.float32), axis=2).T
    grad_weights = jnp.einsum(
        "qhe,jkhe->jhqk", grad_heads, all_values, preferred_element_type=jnp.float32
    )
    grad_scores = (weights_full * (grad_weights - row_delta[None, :, :, None]) * inv_root).astype(
        jnp.bfloat16
    )
    grad_queries = jnp.einsum(
        "jhqk,jkhe->qhe", grad_scores, all_keys, preferred_element_type=jnp.float32
    )
    grad_queries = grad_queries.astype(jnp.bfloat16).reshape(tok_rows, model_width)
    near_q, near_g = shifted((queries, grad_out), "tile", 1)
    near_lse, near_delta = shifted((log_total, row_delta), "tile", 1)
    past_q, past_g, prev_q, prev_g = (
        lax.all_gather(queries[None], "tm", axis=0, tiled=True),
        lax.all_gather(grad_out[None], "tm", axis=0, tiled=True),
        lax.all_gather(near_q[None], "tm", axis=0, tiled=True),
        lax.all_gather(near_g[None], "tm", axis=0, tiled=True),
    )
    past_lse, past_delta, prev_lse, prev_delta = (
        lax.all_gather(log_total[None], "tm", axis=0, tiled=True),
        lax.all_gather(row_delta[None], "tm", axis=0, tiled=True),
        lax.all_gather(near_lse[None], "tm", axis=0, tiled=True),
        lax.all_gather(near_delta[None], "tm", axis=0, tiled=True),
    )
    source_q = jnp.concatenate([past_q, prev_q], axis=1).reshape(
        groups, 2 * tok_rows, head_count, head_width
    )
    source_g = jnp.concatenate([past_g, prev_g], axis=1).reshape(
        groups, 2 * tok_rows, head_count, head_width
    )
    source_lse = jnp.concatenate([past_lse, prev_lse], axis=2)
    source_delta = jnp.concatenate([past_delta, prev_delta], axis=2)
    prev_tile = (my_tile + tile_count - 1) % tile_count
    tile_ids = jnp.arange(tile_count, dtype=jnp.int32)
    prev_live = jnp.sum(jnp.where(tile_ids[None, :] == prev_tile, live_table, 0), axis=1)
    seen_by = own_span <= span_of_group
    query_mask = seen_by[:, None] & (first_half[None, :] | (prev_live[:, None] == 1))
    my_bias = jnp.sum(jnp.where(group_ids[:, None] == my_group, group_bias, 0.0), axis=0)
    key_heads = keys.reshape(tok_rows, head_count, head_width)
    value_heads = values.reshape(tok_rows, head_count, head_width)
    back_scores = jnp.einsum(
        "gqhe,khe->ghqk", source_q, key_heads, preferred_element_type=jnp.float32
    )
    back_scores = back_scores * inv_root + my_bias[None, :, None, None]
    back_full = jnp.where(
        query_mask[:, None, :, None], jnp.exp(back_scores - source_lse[:, :, :, None]), 0.0
    )
    back_low = back_full.astype(jnp.bfloat16)
    back_grad = jnp.einsum(
        "gqhe,khe->ghqk", source_g, value_heads, preferred_element_type=jnp.float32
    )
    back_ds = (back_full * (back_grad - source_delta[:, :, :, None]) * inv_root).astype(
        jnp.bfloat16
    )
    grad_keys = jnp.einsum("ghqk,gqhe->khe", back_ds, source_q, preferred_element_type=jnp.float32)
    grad_values = jnp.einsum(
        "ghqk,gqhe->khe", back_low, source_g, preferred_element_type=jnp.float32
    )
    grad_keys = grad_keys.astype(jnp.bfloat16).reshape(tok_rows, model_width)
    grad_values = grad_values.astype(jnp.bfloat16).reshape(tok_rows, model_width)
    return (attended.reshape(tok_rows, model_width), grad_queries, grad_keys, grad_values)


def solution(mesh):
    in_specs = (
        P(("tm", "tile"), None),
        P(("tm", "tile"), None),
        P(("tm", "tile"), None),
        P(("tm", "tile"), None),
        P(),
        P(),
        P(),
        P(),
    )
    out_specs = (
        P(("tm", "tile"), None),
        P(("tm", "tile"), None),
        P(("tm", "tile"), None),
        P(("tm", "tile"), None),
    )
    return jax.shard_map(
        per_device, mesh=mesh, in_specs=in_specs, out_specs=out_specs, check_vma=False
    )
```

profile of v0, /device:TPU:0, one launch (start us, length us, event | category | flops | bytes accessed | tf_op | source)
XLA Modules:
  0.0 683.0 jit_solution(12979468806883609917)
XLA Ops:
  8.0 3.6 collective-permute-start
  11.6 5.6 collective-permute-done
  18.7 3.0 collective-permute-start.1
  21.8 5.6 collective-permute-done.1
  28.8 9.1 %collective-permute-done.4 = bf16[128,1536]{1,0:T(8,128)(2,1)S(1)} collective-permute-done((bf16[128,1536]{1,0:T(8,128)(2,1)}, bf16[128,1536]{1,0:T(8,128)(2,1)S(1)}, u32[]{:S(2)}, u32[]{:S(2)}) %collective-permute-start.4) | collective-permute-done | bytes 393248 | tf_op jit(solution)/shard_map/ppermute | solution.py:10
  52.0 21.8 %all-gather.25.cloned.1.call-done = bf16[2048,1536]{1,0:T(8,128)(2,1)} async-done(((bf16[128,1536]{1,0:T(8,128)(2,1)}), bf16[2048,1536]{1,0:T(8,128)(2,1)}) %all-gather.25.cloned.1.call-update) | async-done | bytes 6291472 | tf_op jit(solution)/shard_map/all_gather | solution.py:46
  73.8 63.6 %all-gather.27.cloned.1.call-done = bf16[2048,1536]{1,0:T(8,128)(2,1)} async-done(((bf16[128,1536]{1,0:T(8,128)(2,1)}), bf16[2048,1536]{1,0:T(8,128)(2,1)}) %all-gather.27.cloned.1.call-update) | async-done | bytes 6291472 | tf_op jit(solution)/shard_map/all_gather | solution.py:48
  137.4 10.5 %pad_maximum_fusion = bf16[16,256,1536]{2,1,0:T(8,128)(2,1)} fusion(bf16[16,128,1536]{2,1,0:T(8,128)(2,1)} %bitcast.126, bf16[16,128,1536]{2,1,0:T(8,128)(2,1)} %bitcast.122), kind=kLoop, calls=%fused_computation.16 | loop fusion | flops 25165824 | bytes 25165824 | tf_op jit(solution)/shard_map/concatenate | solution.py:53
  147.9 16.7 %copy.101 = bf16[16,256,1536]{1,2,0:T(8,128)(2,1)} copy(bf16[16,256,1536]{2,1,0:T(8,128)(2,1)} %pad_maximum_fusion) | data formatting | bytes 25165824 | tf_op jit(solution)/shard_map/concatenate | solution.py:53
  164.6 35.8 %all-gather.29.cloned.1.call-done = bf16[2048,1536]{1,0:T(8,128)(2,1)} async-done(((bf16[128,1536]{1,0:T(8,128)(2,1)}), bf16[2048,1536]{1,0:T(8,128)(2,1)}) %all-gather.29.cloned.1.call-update) | async-done | bytes 6291472 | tf_op jit(solution)/shard_map/all_gather | solution.py:45
  200.4 63.5 %all-gather.31.cloned.1.call-done = bf16[2048,1536]{1,0:T(8,128)(2,1)} async-done(((bf16[128,1536]{1,0:T(8,128)(2,1)}), bf16[2048,1536]{1,0:T(8,128)(2,1)}) %all-gather.31.cloned.1.call-update) | async-done | bytes 6291472 | tf_op jit(solution)/shard_map/all_gather | solution.py:47
  263.9 10.5 %pad_maximum_fusion.1 = bf16[16,256,1536]{2,1,0:T(8,128)(2,1)} fusion(bf16[16,128,1536]{2,1,0:T(8,128)(2,1)} %bitcast.128, bf16[16,128,1536]{2,1,0:T(8,128)(2,1)} %bitcast.125), kind=kLoop, calls=%fused_computation.17 | loop fusion | flops 25165824 | bytes 25165824 | tf_op jit(solution)/shard_map/concatenate | solution.py:50
  274.3 16.7 %copy.102 = bf16[16,256,1536]{1,2,0:T(8,128)(2,1)} copy(bf16[16,256,1536]{2,1,0:T(8,128)(2,1)} %pad_maximum_fusion.1) | data formatting | bytes 25165824 | tf_op jit(solution)/shard_map/concatenate | solution.py:50
  291.1 15.8 %fusion.26 = (f32[12,128]{1,0:T(8,128)S(1)}, f32[12,16,256,128]{3,2,1,0:T(8,128)}) fusion(f32[16,12]{0,1:T(8,128)S(1)} %copy.106, pred[16,256]{1,0:T(8,128)(4,1)S(1)} %broadcast_and_fusion, bf16[128,12,128,1]{0,2,3,1:T(8,128)(2,1)S(1)} %bitcast.134, bf16[16,256,12,128]{1,3,2,0:T(8,128)(2,1)} %bitcast.118), kind=kOutput, calls=%fused_computation.36 | convolution fusion | flops 1635777024 | bytes 38152960 | tf_op jit(solution)/shard_map/qhe,jkhe->jhqk/dot_general | solution.py:58
  306.9 12.4 %exponential_reduce_fusion = f32[12,128]{1,0:T(8,128)S(1)} fusion(f32[12,128]{1,0:T(8,128)S(1)} %get-tuple-element.28, f32[16,12]{0,1:T(8,128)S(1)} %copy.106, f32[12,16,256,128]{3,2,1,0:T(8,128)} %get-tuple-element.29, pred[16,256]{1,0:T(8,128)(4,1)S(1)} %broadcast_and_fusion), kind=kLoop, calls=%fused_computation.13 | loop fusion | flops 31455744 | bytes 25182976 | tf_op jit(solution)/shard_map/reduce_sum | solution.py:63
  319.3 16.1 %multiply_reduce_fusion = (f32[128,12]{0,1:T(8,128)S(1)}, bf16[12,128,128]{2,1,0:T(8,128)(2,1)S(1)}) fusion(bf16[128,12,128]{0,2,1:T(8,128)(2,1)S(1)} %bitcast.132, bf16[16,256,12,128]{1,3,2,0:T(8,128)(2,1)} %bitcast.116, f32[12,128]{1,0:T(8,128)S(1)} %log_add_fusion, f32[16,12]{0,1:T(8,128)S(1)} %copy.106, f32[12,16,256,128]{3,2,1,0:T(8,128)} %get-tuple-element.29, ...), kind=kOutput, calls=%fused_computation.45 | convolution fusion | flops 1643051520 | bytes 38552320 | tf_op jit(solution)/shard_map/jhqk,jkhe->qhe/dot_general | solution.py:67
  337.0 53.2 %all-gather.39.cloned.1.call-done = bf16[2048,1536]{1,0:T(8,128)(2,1)} async-done(((bf16[128,1536]{1,0:T(8,128)(2,1)}), bf16[2048,1536]{1,0:T(8,128)(2,1)}) %all-gather.39.cloned.1.call-update) | async-done | bytes 6291472 | tf_op jit(solution)/shard_map/all_gather | solution.py:87
  390.2 10.5 %pad_maximum_fusion.3 = bf16[16,256,1536]{2,1,0:T(8,128)(2,1)} fusion(bf16[16,128,1536]{2,1,0:T(8,128)(2,1)} %bitcast.127, bf16[16,128,1536]{2,1,0:T(8,128)(2,1)} %bitcast.123), kind=kLoop, calls=%fused_computation.19 | loop fusion | flops 25165824 | bytes 25165824 | tf_op jit(solution)/shard_map/concatenate | solution.py:98
  400.7 15.9 %copy.117 = bf16[16,256,1536]{1,2,0:T(8,128)(2,1)} copy(bf16[16,256,1536]{2,1,0:T(8,128)(2,1)} %pad_maximum_fusion.3) | data formatting | bytes 25165824 | tf_op jit(solution)/shard_map/concatenate | solution.py:98
  416.5 24.4 %all-gather.12 = f32[16,12,128]{2,1,0:T(8,128)S(1)} all-gather(f32[1,12,128]{2,1,0:T(8,128)S(1)} %bitcast.139), channel_id=8, replica_groups=mesh['tm'=16,'tile'=8] {'tm'}, dimensions={0}, use_global_device_ids=true | all-gather | bytes 104448 | tf_op jit(solution)/shard_map/all_gather | solution.py:90
  440.9 21.8 %fusion.6 = bf16[16,12,128,256]{2,3,0,1:T(8,128)(2,1)} fusion(f32[12,128]{1,0:T(8,128)S(1)} %bitcast.142, f32[12,128]{1,0:T(8,128)S(1)} %log_add_fusion, f32[16,12]{0,1:T(8,128)S(1)} %copy.106, f32[12,16,256,128]{3,2,1,0:T(8,128)} %get-tuple-element.29, pred[16,256]{1,0:T(8,128)(4,1)S(1)} %broadcast_and_fusion, bf16[128,12,128,1]{0,2,3,1:T(8,128)(2,1)S(1)} %bitcast.133, ...), kind=kOutput, calls=%fused_computation.9 | convolution fusion | flops 1660944384 | bytes 50742016 | tf_op jit(solution)/shard_map/qhe,jkhe->jhqk/dot_general | solution.py:71
  462.7 12.0 %fusion.39 = bf16[12,128,128]{2,1,0:T(8,128)(2,1)S(1)} fusion(bf16[16,256,12,128]{1,3,2,0:T(8,128)(2,1)} %bitcast.119, bf16[16,12,128,256]{2,3,0,1:T(8,128)(2,1)} %fusion.6), kind=kOutput, calls=%fused_computation.41 | convolution fusion | flops 1610809344 | bytes 25559040 | tf_op jit(solution)/shard_map/jhqk,jkhe->qhe/dot_general | solution.py:77
  474.7 42.6 %all-gather.35.cloned.1.call-done = bf16[2048,1536]{1,0:T(8,128)(2,1)} async-done(((bf16[128,1536]{1,0:T(8,128)(2,1)}), bf16[2048,1536]{1,0:T(8,128)(2,1)}) %all-gather.35.cloned.1.call-update) | async-done | bytes 6291472 | tf_op jit(solution)/shard_map/all_gather | solution.py:86
  517.3 10.4 %pad_maximum_fusion.2 = bf16[16,256,1536]{2,1,0:T(8,128)(2,1)} fusion(bf16[16,128,1536]{2,1,0:T(8,128)(2,1)} %bitcast.129, bf16[16,128,1536]{2,1,0:T(8,128)(2,1)} %bitcast.124), kind=kLoop, calls=%fused_computation.18 | loop fusion | flops 25165824 | bytes 25165824 | tf_op jit(solution)/shard_map/concatenate | solution.py:95
  527.8 13.1 %fusion.10 = f32[12,16,256,128]{3,2,1,0:T(8,128)} fusion(bf16[128,12,128,1]{0,2,3,1:T(8,128)(2,1)S(1)} %bitcast.130, bf16[16,256,12,128]{1,3,2,0:T(8,128)(2,1)} %bitcast.114), kind=kOutput, calls=%fused_computation.20 | convolution fusion | flops 1610612736 | bytes 38141952 | tf_op jit(solution)/shard_map/gqhe,khe->ghqk/dot_general | solution.py:119
  540.9 23.3 %all-gather.14 = f32[16,12,128]{2,1,0:T(8,128)S(1)} all-gather(f32[1,12,128]{2,1,0:T(8,128)S(1)} %bitcast.143), channel_id=12, replica_groups=mesh['tm'=16,'tile'=8] {'tm'}, dimensions={0}, use_global_device_ids=true | all-gather | bytes 104448 | tf_op jit(solution)/shard_map/all_gather | solution.py:91
  566.1 16.6 %copy.112 = bf16[16,256,1536]{1,2,0:T(8,128)(2,1)} copy(bf16[16,256,1536]{2,1,0:T(8,128)(2,1)} %pad_maximum_fusion.2) | data formatting | bytes 25165824 | tf_op jit(solution)/shard_map/concatenate | solution.py:95
  582.7 21.5 %all-gather.13 = f32[16,12,128]{2,1,0:T(8,128)S(1)} all-gather(f32[1,12,128]{2,1,0:T(8,128)S(1)} %bitcast.144), channel_id=9, replica_groups=mesh['tm'=16,'tile'=8] {'tm'}, dimensions={0}, use_global_device_ids=true | all-gather | bytes 104448 | tf_op jit(solution)/shard_map/all_gather | solution.py:92
  604.4 23.3 %all-gather.15 = f32[16,12,128]{2,1,0:T(8,128)S(1)} all-gather(f32[1,12,128]{2,1,0:T(8,128)S(1)} %bitcast.140), channel_id=13, replica_groups=mesh['tm'=16,'tile'=8] {'tm'}, dimensions={0}, use_global_device_ids=true | all-gather | bytes 104448 | tf_op jit(solution)/shard_map/all_gather | solution.py:93
  627.8 23.3 %fusion.9 = (bf16[16,12,256,128]{3,2,0,1:T(8,128)(2,1)}, bf16[16,12,256,128]{3,2,0,1:T(8,128)(2,1)}) fusion(f32[16,12,256]{2,0,1:T(8,128)S(1)} %copy.116, f32[12]{0:T(128)S(1)} %get-tuple-element.32, pred[16,256]{1,0:T(8,128)(4,1)S(1)} %or_and_fusion, f32[16,12,256]{2,0,1:T(8,128)S(1)} %copy.121, f32[12,16,256,128]{3,2,1,0:T(8,128)} %fusion.10, ...), kind=kOutput, calls=%fused_computation.15 | convolution fusion | flops 1667235840 | bytes 63705136 | tf_op jit(solution)/shard_map/gqhe,khe->ghqk/dot_general | solution.py:111
  651.1 11.6 %fusion.48 = bf16[12,128,128]{2,1,0:T(8,128)(2,1)S(1)} fusion(bf16[16,256,12,128]{1,3,2,0:T(8,128)(2,1)} %bitcast.121, bf16[16,12,256,128]{3,2,0,1:T(8,128)(2,1)} %get-tuple-element.25), kind=kOutput, calls=%fused_computation.44 | convolution fusion | flops 1610809344 | bytes 25559040 | tf_op jit(solution)/shard_map/ghqk,gqhe->khe/dot_general | solution.py:125
  663.6 11.6 %fusion.45 = bf16[12,128,128]{2,1,0:T(8,128)(2,1)S(1)} fusion(bf16[16,256,12,128]{1,3,2,0:T(8,128)(2,1)} %bitcast.115, bf16[16,12,256,128]{3,2,0,1:T(8,128)(2,1)} %get-tuple-element.24), kind=kOutput, calls=%fused_computation.43 | convolution fusion | flops 1610809344 | bytes 25559040 | tf_op jit(solution)/shard_map/ghqk,gqhe->khe/dot_general | solution.py:126
  (65 shorter events, 22.7 us)
Async XLA Ops:
  7.2 38.1 %copy-start = (f32[1000,12]{0,1:T(8,128)S(1)}, f32[1000,12]{0,1:T(8,128)}, u32[]{:S(2)}) copy-start(f32[1000,12]{0,1:T(8,128)} %param.15) | copy-start | bytes 144004
  7.2 66.6 %all-gather.25.cloned.1.call-start = ((), (), s32[]{:S(2)}) async-start(), calls=%async_computation | async-start | bytes 6684672 | tf_op jit(solution)/shard_map/all_gather | solution.py:46
  7.9 129.5 %all-gather.27.cloned.1.call-start = ((), (), s32[]{:S(2)}) async-start(), calls=%async_computation.1 | async-start | bytes 6684672 | tf_op jit(solution)/shard_map/all_gather | solution.py:48
  8.0 9.2 %collective-permute-start = (bf16[128,1536]{1,0:T(8,128)(2,1)}, bf16[128,1536]{1,0:T(8,128)(2,1)S(1)}, u32[]{:S(2)}, u32[]{:S(2)}) collective-permute-start(bf16[128,1536]{1,0:T(8,128)(2,1)} %param.10), channel_id=1, source_target_pairs={{0,7},{1,0},{2,1},{3,2},{4,3},{5,4},{6,5},{7,6},{8,15},{9,8},{10,9... | collective-permute-start | bytes 1179656 | tf_op jit(solution)/shard_map/ppermute | solution.py:10
  17.2 0.7 copy-start.2
  17.9 182.5 %all-gather.29.cloned.1.call-start = ((), (), s32[]{:S(2)}) async-start(), calls=%async_computation.2 | async-start | bytes 6684672 | tf_op jit(solution)/shard_map/all_gather | solution.py:45
  18.7 245.2 %all-gather.31.cloned.1.call-start = ((), (), s32[]{:S(2)}) async-start(), calls=%async_computation.3 | async-start | bytes 6684672 | tf_op jit(solution)/shard_map/all_gather | solution.py:47
  18.7 8.6 %collective-permute-start.1 = (bf16[128,1536]{1,0:T(8,128)(2,1)}, bf16[128,1536]{1,0:T(8,128)(2,1)S(1)}, u32[]{:S(2)}, u32[]{:S(2)}) collective-permute-start(bf16[128,1536]{1,0:T(8,128)(2,1)} %param.9), channel_id=1, source_target_pairs={{0,7},{1,0},{2,1},{3,2},{4,3},{5,4},{6,5},{7,6},{8,15},{9,8},{10,9... | collective-permute-start | bytes 1179656 | tf_op jit(solution)/shard_map/ppermute | solution.py:10
  27.4 0.7 copy-start.5
  28.1 308.9 %all-gather.37.cloned.1.call-start = ((), (), s32[]{:S(2)}) async-start(), calls=%async_computation.6 | async-start | bytes 6684672 | tf_op jit(solution)/shard_map/all_gather | solution.py:85
  28.7 361.5 %all-gather.39.cloned.1.call-start = ((), (), s32[]{:S(2)}) async-start(), calls=%async_computation.7 | async-start | bytes 6684672 | tf_op jit(solution)/shard_map/all_gather | solution.py:87
  28.8 9.1 %collective-permute-start.4 = (bf16[128,1536]{1,0:T(8,128)(2,1)}, bf16[128,1536]{1,0:T(8,128)(2,1)S(1)}, u32[]{:S(2)}, u32[]{:S(2)}) collective-permute-start(bf16[128,1536]{1,0:T(8,128)(2,1)} %param.11), channel_id=1, source_target_pairs={{0,1},{1,2},{2,3},{3,4},{4,5},{5,6},{6,7},{7,0},{8,9},{9,10},{10,1... | collective-permute-start | bytes 1179656 | tf_op jit(solution)/shard_map/ppermute | solution.py:10
  37.9 0.7 copy-start.3
  38.6 436.1 %all-gather.33.cloned.1.call-start = ((), (), s32[]{:S(2)}) async-start(), calls=%async_computation.4 | async-start | bytes 6684672 | tf_op jit(solution)/shard_map/all_gather | solution.py:84
  39.4 478.0 %all-gather.35.cloned.1.call-start = ((), (), s32[]{:S(2)}) async-start(), calls=%async_computation.5 | async-start | bytes 6684672 | tf_op jit(solution)/shard_map/all_gather | solution.py:86
  39.4 11.8 %collective-permute-start.2 = (bf16[128,1536]{1,0:T(8,128)(2,1)}, bf16[128,1536]{1,0:T(8,128)(2,1)S(1)}, u32[]{:S(2)}, u32[]{:S(2)}) collective-permute-start(bf16[128,1536]{1,0:T(8,128)(2,1)} %param.8), channel_id=1, source_target_pairs={{0,1},{1,2},{2,3},{3,4},{4,5},{5,6},{6,7},{7,0},{8,9},{9,10},{10,1... | collective-permute-start | bytes 1179656 | tf_op jit(solution)/shard_map/ppermute | solution.py:10
  51.2 0.7 copy-start.4
  319.3 263.5 %collective-permute-start.3 = (f32[12,128]{1,0:T(8,128)S(1)}, f32[12,128]{1,0:T(8,128)S(1)}, u32[]{:S(2)}, u32[]{:S(2)}) collective-permute-start(f32[12,128]{1,0:T(8,128)S(1)} %log_add_fusion), channel_id=1, source_target_pairs={{0,1},{1,2},{2,3},{3,4},{4,5},{5,6},{6,7},{7,0},{8,9},{9,10},{10,1... | collective-permute-start | bytes 18440 | tf_op jit(solution)/shard_map/ppermute | solution.py:10
  335.4 269.0 %collective-permute-start.5 = (f32[12,128]{1,0:T(8,128)S(1)}, f32[12,128]{1,0:T(8,128)S(1)}, u32[]{:S(2)}, u32[]{:S(2)}) collective-permute-start(f32[12,128]{1,0:T(8,128)S(1)} %bitcast.141), channel_id=1, source_target_pairs={{0,1},{1,2},{2,3},{3,4},{4,5},{5,6},{6,7},{7,0},{8,9},{9,10},{10,1... | collective-permute-start | bytes 18440 | tf_op jit(solution)/shard_map/ppermute | solution.py:10
  663.6 12.6 %copy-start.1 = (f32[1000,12]{0,1:T(8,128)S(1)}, f32[1000,12]{0,1:T(8,128)}, u32[]{:S(2)}) copy-start(f32[1000,12]{0,1:T(8,128)} %param.15) | copy-start | bytes 144004
Sparse Core Ops, SparseCore 0:
  10.1 63.6 all-gather.24
  76.5 60.8 all-gather.26
  139.5 60.8 all-gather.28
  203.0 60.8 all-gather.30
  265.8 60.8 all-gather.36
  329.3 60.8 all-gather.38
  392.3 61.3 all-gather.32
  456.5 60.8 all-gather.34
where the time goes:
time: 685 us; the launch traced here: 683 us
  waiting for transfers between devices  303 us (44%)
  matrix products  125 us (18%)
  blocking collectives  92.5 us (14%)
  local copies, waits for them, and re-layouts  78.6 us (11%)
  other arithmetic  59.4 us (9%)
  between operations  15 us (2%)
  starting transfers between devices  8.61 us (1%)
    all_gather x1, waiting for transfers between devices, per_device(): lax.all_gather(near_v[None], 'tm', axis=0, tiled=True)  63.6 us
    all_gather x1, waiting for transfers between devices, per_device(): lax.all_gather(near_k[None], 'tm', axis=0, tiled=True)  63.5 us
    all_gather x1, waiting for transfers between devices, per_device(): lax.all_gather(near_g[None], 'tm', axis=0, tiled=True)  53.2 us
    all_gather x1, waiting for transfers between devices, per_device(): lax.all_gather(near_q[None], 'tm', axis=0, tiled=True)  42.6 us
    all_gather x1, waiting for transfers between devices, per_device(): lax.all_gather(keys[None], 'tm', axis=0, tiled=True)  35.8 us
    all_gather x1, blocking collectives, per_device(): lax.all_gather(log_total[None], 'tm', axis=0, tiled=True)  24.4 us
    all_gather x1, blocking collectives, per_device(): lax.all_gather(row_delta[None], 'tm', axis=0, tiled=True)  23.3 us
    all_gather x1, blocking collectives, per_device(): lax.all_gather(near_delta[None], 'tm', axis=0, tiled=True)  23.3 us
  transfers between devices with their start and end apart: 14, of which 9 were waited for; matrix products, arithmetic and copies ran while one was open for 31% of the time, Pallas kernels for 0%

commit v1 on v0

--- a/solution.py
+++ b/solution.py
@@ -3,6 +3,11 @@
 import jax.numpy as jnp
 from jax import lax
 from jax.sharding import PartitionSpec as P
+
+
+def gather_from_all(x, axis, dim):
+    copies = jnp.concatenate([x] * lax.axis_size(axis), axis=dim)
+    return lax.all_to_all(copies, axis, dim, dim, tiled=True)
 
 
 def shifted(value, axis, by):
@@ -43,7 +48,7 @@
     near_k, near_v = shifted((keys, values), "tile", -1)
     past_k, past_v, ahead_k, ahead_v = (
         lax.all_gather(keys[None], "tm", axis=0, tiled=True),
-        lax.all_gather(values[None], "tm", axis=0, tiled=True),
+        gather_from_all(values[None], "tm", 0),
         lax.all_gather(near_k[None], "tm", axis=0, tiled=True),
         lax.all_gather(near_v[None], "tm", axis=0, tiled=True),
     )

time: 685 us -> 696 us (1.016)
  waiting for transfers between devices: 303 us -> 310 us
  starting transfers between devices: 8.61 us -> 15.6 us
    all_to_all x0 -> x1, waiting for transfers between devices: none -> 88.4 us  [gather_from_all(): return lax.all_to_all(copies, axis, dim, dim, tiled=True)]
    all_gather x1, waiting for transfers between devices: 63.6 us -> 0.01 us  [per_device(): lax.all_gather(near_v[None], 'tm', axis=0, tiled=True)]
    all_gather x1 -> x0, waiting for transfers between devices: 21.8 us -> none  [per_device(): lax.all_gather(values[None], 'tm', axis=0, tiled=True)]
    all_to_all x0 -> x1, starting transfers between devices: none -> 7.08 us  [gather_from_all(): return lax.all_to_all(copies, axis, dim, dim, tiled=True)]
  transfers between devices with their start and end apart: 14 -> 14, of which waited for: 9 -> 9; matrix products, arithmetic and copies ran while one was open for 31% -> 30% of each run, Pallas kernels for 0% -> 0%
where the time goes in v1:
time: 696 us; the launch traced here: 694 us
  waiting for transfers between devices  310 us (45%)
  matrix products  125 us (18%)
  blocking collectives  93 us (13%)
  local copies, waits for them, and re-layouts  78.1 us (11%)
  other arithmetic  56.6 us (8%)
  starting transfers between devices  15.6 us (2%)
  between operations  15.1 us (2%)
    all_to_all x1, waiting for transfers between devices, gather_from_all(): return lax.all_to_all(copies, axis, dim, dim, tiled=True)  88.4 us
    all_gather x1, waiting for transfers between devices, per_device(): lax.all_gather(near_k[None], 'tm', axis=0, tiled=True)  63.6 us
    all_gather x1, waiting for transfers between devices, per_device(): lax.all_gather(near_g[None], 'tm', axis=0, tiled=True)  53.3 us
    all_gather x1, waiting for transfers between devices, per_device(): lax.all_gather(near_q[None], 'tm', axis=0, tiled=True)  42 us
    all_gather x1, waiting for transfers between devices, per_device(): lax.all_gather(keys[None], 'tm', axis=0, tiled=True)  37.2 us
    all_gather x1, blocking collectives, per_device(): lax.all_gather(log_total[None], 'tm', axis=0, tiled=True)  24.9 us
    ppermute x6, waiting for transfers between devices, shifted(): lax.ppermute(value, axis, [(i, (i + by) % count) for i in range(count)])  23.8 us
    all_gather x1, blocking collectives, per_device(): lax.all_gather(row_delta[None], 'tm', axis=0, tiled=True)  23.3 us
  transfers between devices with their start and end apart: 14, of which 9 were waited for; matrix products, arithmetic and copies ran while one was open for 30% of the time, Pallas kernels for 0%

profile of v1, /device:TPU:0, one launch (start us, length us, event | category | flops | bytes accessed | tf_op | source)
XLA Modules:
  0.0 694.1 jit_solution(11319764645234005324)
XLA Ops:
  10.9 5.6 collective-permute-done
  21.1 5.6 collective-permute-done.1
  28.1 8.7 %collective-permute-done.4 = bf16[128,1536]{1,0:T(8,128)(2,1)S(1)} collective-permute-done((bf16[128,1536]{1,0:T(8,128)(2,1)}, bf16[128,1536]{1,0:T(8,128)(2,1)S(1)}, u32[]{:S(2)}, u32[]{:S(2)}) %collective-permute-start.4) | collective-permute-done | bytes 393248 | tf_op jit(solution)/shard_map/ppermute | solution.py:15
  38.2 4.3 concatenate.21
  42.4 7.1 %all-to-all-start = ((bf16[16,128,1536]{2,1,0:T(8,128)(2,1)}), bf16[16,128,1536]{2,1,0:T(8,128)(2,1)}, u32[]{:S(2)}, u32[]{:S(2)}) async-start(bf16[16,128,1536]{2,1,0:T(8,128)(2,1)} %concatenate.21), calls=%async_computation | async-start | bytes 12582912 | tf_op jit(solution)/shard_map/all_to_all | solution.py:10
  54.1 3.9 collective-permute-done.2
  58.8 88.4 %all-to-all-done = bf16[16,128,1536]{2,1,0:T(8,128)(2,1)} async-done(((bf16[16,128,1536]{2,1,0:T(8,128)(2,1)}), bf16[16,128,1536]{2,1,0:T(8,128)(2,1)}, u32[]{:S(2)}, u32[]{:S(2)}) %all-to-all-start) | async-done | bytes 6291488 | tf_op jit(solution)/shard_map/all_to_all | solution.py:10
  147.2 10.4 %pad_maximum_fusion = bf16[16,256,1536]{2,1,0:T(8,128)(2,1)} fusion(bf16[16,128,1536]{2,1,0:T(8,128)(2,1)} %bitcast.124, bf16[16,128,1536]{2,1,0:T(8,128)(2,1)} %all-to-all-done), kind=kLoop, calls=%fused_computation.16 | loop fusion | flops 25165824 | bytes 25165824 | tf_op jit(solution)/shard_map/concatenate | solution.py:58
  157.6 16.7 %copy.102 = bf16[16,256,1536]{1,2,0:T(8,128)(2,1)} copy(bf16[16,256,1536]{2,1,0:T(8,128)(2,1)} %pad_maximum_fusion) | data formatting | bytes 25165824 | tf_op jit(solution)/shard_map/concatenate | solution.py:58
  174.3 37.2 %all-gather.25.cloned.1.call-done = bf16[2048,1536]{1,0:T(8,128)(2,1)} async-done(((bf16[128,1536]{1,0:T(8,128)(2,1)}), bf16[2048,1536]{1,0:T(8,128)(2,1)}) %all-gather.25.cloned.1.call-update) | async-done | bytes 6291472 | tf_op jit(solution)/shard_map/all_gather | solution.py:50
  211.5 63.6 %all-gather.27.cloned.1.call-done = bf16[2048,1536]{1,0:T(8,128)(2,1)} async-done(((bf16[128,1536]{1,0:T(8,128)(2,1)}), bf16[2048,1536]{1,0:T(8,128)(2,1)}) %all-gather.27.cloned.1.call-update) | async-done | bytes 6291472 | tf_op jit(solution)/shard_map/all_gather | solution.py:52
  275.1 10.4 %pad_maximum_fusion.1 = bf16[16,256,1536]{2,1,0:T(8,128)(2,1)} fusion(bf16[16,128,1536]{2,1,0:T(8,128)(2,1)} %bitcast.126, bf16[16,128,1536]{2,1,0:T(8,128)(2,1)} %bitcast.123), kind=kLoop, calls=%fused_computation.17 | loop fusion | flops 25165824 | bytes 25165824 | tf_op jit(solution)/shard_map/concatenate | solution.py:55
  285.6 16.7 %copy.103 = bf16[16,256,1536]{1,2,0:T(8,128)(2,1)} copy(bf16[16,256,1536]{2,1,0:T(8,128)(2,1)} %pad_maximum_fusion.1) | data formatting | bytes 25165824 | tf_op jit(solution)/shard_map/concatenate | solution.py:55
  302.3 15.8 %fusion.26 = (f32[12,128]{1,0:T(8,128)S(1)}, f32[12,16,256,128]{3,2,1,0:T(8,128)}) fusion(f32[16,12]{0,1:T(8,128)S(1)} %copy.107, pred[16,256]{1,0:T(8,128)(4,1)S(1)} %broadcast_and_fusion, bf16[128,12,128,1]{0,2,3,1:T(8,128)(2,1)S(1)} %bitcast.132, bf16[16,256,12,128]{1,3,2,0:T(8,128)(2,1)} %bitcast.117), kind=kOutput, calls=%fused_computation.36 | convolution fusion | flops 1635777024 | bytes 38152960 | tf_op jit(solution)/shard_map/qhe,jkhe->jhqk/dot_general | solution.py:63
  318.0 12.4 %exponential_reduce_fusion = f32[12,128]{1,0:T(8,128)S(1)} fusion(f32[12,128]{1,0:T(8,128)S(1)} %get-tuple-element.28, f32[16,12]{0,1:T(8,128)S(1)} %copy.107, f32[12,16,256,128]{3,2,1,0:T(8,128)} %get-tuple-element.29, pred[16,256]{1,0:T(8,128)(4,1)S(1)} %broadcast_and_fusion), kind=kLoop, calls=%fused_computation.13 | loop fusion | flops 31455744 | bytes 25182976 | tf_op jit(solution)/shard_map/reduce_sum | solution.py:68
  330.4 16.1 %multiply_reduce_fusion = (f32[128,12]{0,1:T(8,128)S(1)}, bf16[12,128,128]{2,1,0:T(8,128)(2,1)S(1)}) fusion(bf16[128,12,128]{0,2,1:T(8,128)(2,1)S(1)} %bitcast.130, bf16[16,256,12,128]{1,3,2,0:T(8,128)(2,1)} %bitcast.115, f32[12,128]{1,0:T(8,128)S(1)} %log_add_fusion, f32[16,12]{0,1:T(8,128)S(1)} %copy.107, f32[12,16,256,128]{3,2,1,0:T(8,128)} %get-tuple-element.29, ...), kind=kOutput, calls=%fused_computation.45 | convolution fusion | flops 1643051520 | bytes 38552320 | tf_op jit(solution)/shard_map/jhqk,jkhe->qhe/dot_general | solution.py:72
  348.2 53.3 %all-gather.35.cloned.1.call-done = bf16[2048,1536]{1,0:T(8,128)(2,1)} async-done(((bf16[128,1536]{1,0:T(8,128)(2,1)}), bf16[2048,1536]{1,0:T(8,128)(2,1)}) %all-gather.35.cloned.1.call-update) | async-done | bytes 6291472 | tf_op jit(solution)/shard_map/all_gather | solution.py:92
  401.5 10.5 %pad_maximum_fusion.3 = bf16[16,256,1536]{2,1,0:T(8,128)(2,1)} fusion(bf16[16,128,1536]{2,1,0:T(8,128)(2,1)} %bitcast.125, bf16[16,128,1536]{2,1,0:T(8,128)(2,1)} %bitcast.121), kind=kLoop, calls=%fused_computation.19 | loop fusion | flops 25165824 | bytes 25165824 | tf_op jit(solution)/shard_map/concatenate | solution.py:103
  411.9 15.8 %copy.118 = bf16[16,256,1536]{1,2,0:T(8,128)(2,1)} copy(bf16[16,256,1536]{2,1,0:T(8,128)(2,1)} %pad_maximum_fusion.3) | data formatting | bytes 25165824 | tf_op jit(solution)/shard_map/concatenate | solution.py:103
  427.8 24.9 %all-gather.11 = f32[16,12,128]{2,1,0:T(8,128)S(1)} all-gather(f32[1,12,128]{2,1,0:T(8,128)S(1)} %bitcast.137), channel_id=7, replica_groups=mesh['tm'=16,'tile'=8] {'tm'}, dimensions={0}, use_global_device_ids=true | all-gather | bytes 104448 | tf_op jit(solution)/shard_map/all_gather | solution.py:95
  452.7 21.8 %fusion.6 = bf16[16,12,128,256]{2,3,0,1:T(8,128)(2,1)} fusion(f32[12,128]{1,0:T(8,128)S(1)} %bitcast.140, f32[12,128]{1,0:T(8,128)S(1)} %log_add_fusion, f32[16,12]{0,1:T(8,128)S(1)} %copy.107, f32[12,16,256,128]{3,2,1,0:T(8,128)} %get-tuple-element.29, pred[16,256]{1,0:T(8,128)(4,1)S(1)} %broadcast_and_fusion, bf16[128,12,128,1]{0,2,3,1:T(8,128)(2,1)S(1)} %bitcast.131, ...), kind=kOutput, calls=%fused_computation.9 | convolution fusion | flops 1660944384 | bytes 50742016 | tf_op jit(solution)/shard_map/qhe,jkhe->jhqk/dot_general | solution.py:76
  474.5 12.0 %fusion.39 = bf16[12,128,128]{2,1,0:T(8,128)(2,1)S(1)} fusion(bf16[16,256,12,128]{1,3,2,0:T(8,128)(2,1)} %bitcast.118, bf16[16,12,128,256]{2,3,0,1:T(8,128)(2,1)} %fusion.6), kind=kOutput, calls=%fused_computation.41 | convolution fusion | flops 1610809344 | bytes 25559040 | tf_op jit(solution)/shard_map/jhqk,jkhe->qhe/dot_general | solution.py:82
  486.5 42.0 %all-gather.31.cloned.1.call-done = bf16[2048,1536]{1,0:T(8,128)(2,1)} async-done(((bf16[128,1536]{1,0:T(8,128)(2,1)}), bf16[2048,1536]{1,0:T(8,128)(2,1)}) %all-gather.31.cloned.1.call-update) | async-done | bytes 6291472 | tf_op jit(solution)/shard_map/all_gather | solution.py:91
  528.5 10.4 %pad_maximum_fusion.2 = bf16[16,256,1536]{2,1,0:T(8,128)(2,1)} fusion(bf16[16,128,1536]{2,1,0:T(8,128)(2,1)} %bitcast.127, bf16[16,128,1536]{2,1,0:T(8,128)(2,1)} %bitcast.122), kind=kLoop, calls=%fused_computation.18 | loop fusion | flops 25165824 | bytes 25165824 | tf_op jit(solution)/shard_map/concatenate | solution.py:100
  538.9 13.1 %fusion.10 = f32[12,16,256,128]{3,2,1,0:T(8,128)} fusion(bf16[128,12,128,1]{0,2,3,1:T(8,128)(2,1)S(1)} %bitcast.128, bf16[16,256,12,128]{1,3,2,0:T(8,128)(2,1)} %bitcast.113), kind=kOutput, calls=%fused_computation.20 | convolution fusion | flops 1610612736 | bytes 38141952 | tf_op jit(solution)/shard_map/gqhe,khe->ghqk/dot_general | solution.py:124
  552.0 23.3 %all-gather.13 = f32[16,12,128]{2,1,0:T(8,128)S(1)} all-gather(f32[1,12,128]{2,1,0:T(8,128)S(1)} %bitcast.141), channel_id=11, replica_groups=mesh['tm'=16,'tile'=8] {'tm'}, dimensions={0}, use_global_device_ids=true | all-gather | bytes 104448 | tf_op jit(solution)/shard_map/all_gather | solution.py:96
  577.2 16.6 %copy.113 = bf16[16,256,1536]{1,2,0:T(8,128)(2,1)} copy(bf16[16,256,1536]{2,1,0:T(8,128)(2,1)} %pad_maximum_fusion.2) | data formatting | bytes 25165824 | tf_op jit(solution)/shard_map/concatenate | solution.py:100
  593.9 21.5 %all-gather.12 = f32[16,12,128]{2,1,0:T(8,128)S(1)} all-gather(f32[1,12,128]{2,1,0:T(8,128)S(1)} %bitcast.142), channel_id=8, replica_groups=mesh['tm'=16,'tile'=8] {'tm'}, dimensions={0}, use_global_device_ids=true | all-gather | bytes 104448 | tf_op jit(solution)/shard_map/all_gather | solution.py:97
  615.5 23.3 %all-gather.14 = f32[16,12,128]{2,1,0:T(8,128)S(1)} all-gather(f32[1,12,128]{2,1,0:T(8,128)S(1)} %bitcast.138), channel_id=12, replica_groups=mesh['tm'=16,'tile'=8] {'tm'}, dimensions={0}, use_global_device_ids=true | all-gather | bytes 104448 | tf_op jit(solution)/shard_map/all_gather | solution.py:98
  639.0 23.2 %fusion.9 = (bf16[16,12,256,128]{3,2,0,1:T(8,128)(2,1)}, bf16[16,12,256,128]{3,2,0,1:T(8,128)(2,1)}) fusion(f32[16,12,256]{2,0,1:T(8,128)S(1)} %copy.117, f32[12]{0:T(128)S(1)} %get-tuple-element.32, pred[16,256]{1,0:T(8,128)(4,1)S(1)} %or_and_fusion, f32[16,12,256]{2,0,1:T(8,128)S(1)} %copy.122, f32[12,16,256,128]{3,2,1,0:T(8,128)} %fusion.10, ...), kind=kOutput, calls=%fused_computation.15 | convolution fusion | flops 1667235840 | bytes 63705136 | tf_op jit(solution)/shard_map/gqhe,khe->ghqk/dot_general | solution.py:116
  662.2 11.6 %fusion.48 = bf16[12,128,128]{2,1,0:T(8,128)(2,1)S(1)} fusion(bf16[16,256,12,128]{1,3,2,0:T(8,128)(2,1)} %bitcast.120, bf16[16,12,256,128]{3,2,0,1:T(8,128)(2,1)} %get-tuple-element.25), kind=kOutput, calls=%fused_computation.44 | convolution fusion | flops 1610809344 | bytes 25559040 | tf_op jit(solution)/shard_map/ghqk,gqhe->khe/dot_general | solution.py:130
  674.7 11.6 %fusion.45 = bf16[12,128,128]{2,1,0:T(8,128)(2,1)S(1)} fusion(bf16[16,256,12,128]{1,3,2,0:T(8,128)(2,1)} %bitcast.114, bf16[16,12,256,128]{3,2,0,1:T(8,128)(2,1)} %get-tuple-element.24), kind=kOutput, calls=%fused_computation.43 | convolution fusion | flops 1610809344 | bytes 25559040 | tf_op jit(solution)/shard_map/ghqk,gqhe->khe/dot_general | solution.py:131
  (79 shorter events, 21.1 us)
Async XLA Ops:
  7.2 43.6 %copy-start = (f32[1000,12]{0,1:T(8,128)S(1)}, f32[1000,12]{0,1:T(8,128)}, u32[]{:S(2)}) copy-start(f32[1000,12]{0,1:T(8,128)} %param.15) | copy-start | bytes 144004
  7.2 42.9 %copy-start.2 = (bf16[128,1536]{1,0:T(8,128)(2,1)S(1)}, bf16[128,1536]{1,0:T(8,128)(2,1)}, u32[]{:S(2)}) copy-start(bf16[128,1536]{1,0:T(8,128)(2,1)} %param.10) | copy-start | bytes 1179652
  7.2 43.1 %copy-start.3 = (bf16[128,1536]{1,0:T(8,128)(2,1)S(1)}, bf16[128,1536]{1,0:T(8,128)(2,1)}, u32[]{:S(2)}) copy-start(bf16[128,1536]{1,0:T(8,128)(2,1)} %param.9) | copy-start | bytes 1179652
  7.2 42.4 %copy-start.4 = (bf16[128,1536]{1,0:T(8,128)(2,1)S(1)}, bf16[128,1536]{1,0:T(8,128)(2,1)}, u32[]{:S(2)}) copy-start(bf16[128,1536]{1,0:T(8,128)(2,1)} %param.11) | copy-start | bytes 1179652
  7.2 42.3 %copy-start.5 = (bf16[128,1536]{1,0:T(8,128)(2,1)S(1)}, bf16[128,1536]{1,0:T(8,128)(2,1)}, u32[]{:S(2)}) copy-start(bf16[128,1536]{1,0:T(8,128)(2,1)} %param.8) | copy-start | bytes 1179652
  7.2 43.3 %copy-start.12 = (s32[16]{0:T(128)S(1)}, s32[16]{0:T(128)}, u32[]{:S(2)}) copy-start(s32[16]{0:T(128)} %param.13) | copy-start | bytes 196
  7.2 43.3 %copy-start.11 = (s32[16]{0:T(128)S(1)}, s32[16]{0:T(128)}, u32[]{:S(2)}) copy-start(s32[16]{0:T(128)} %param.12) | copy-start | bytes 196
  7.2 43.8 %copy-start.10 = (s32[128]{0:T(128)S(1)}, s32[128]{0:T(128)}, u32[]{:S(2)}) copy-start(s32[128]{0:T(128)} %param.14) | copy-start | bytes 1540
  7.3 139.9 %all-gather.23.cloned.1.call-start = ((), (), s32[]{:S(2)}) async-start(), calls=%async_computation.1 | async-start | bytes 6684672 | tf_op jit(solution)/shard_map/all_gather | solution.py:53
  7.3 9.2 %collective-permute-start = (bf16[128,1536]{1,0:T(8,128)(2,1)}, bf16[128,1536]{1,0:T(8,128)(2,1)S(1)}, u32[]{:S(2)}, u32[]{:S(2)}) collective-permute-start(bf16[128,1536]{1,0:T(8,128)(2,1)} %param.10), channel_id=1, source_target_pairs={{0,7},{1,0},{2,1},{3,2},{4,3},{5,4},{6,5},{7,6},{8,15},{9,8},{10,9... | collective-permute-start | bytes 1179656 | tf_op jit(solution)/shard_map/ppermute | solution.py:15
  16.5 0.7 copy-start.6
  17.3 194.3 %all-gather.25.cloned.1.call-start = ((), (), s32[]{:S(2)}) async-start(), calls=%async_computation.2 | async-start | bytes 6684672 | tf_op jit(solution)/shard_map/all_gather | solution.py:50
  18.0 257.1 %all-gather.27.cloned.1.call-start = ((), (), s32[]{:S(2)}) async-start(), calls=%async_computation.3 | async-start | bytes 6684672 | tf_op jit(solution)/shard_map/all_gather | solution.py:52
  18.1 8.6 %collective-permute-start.1 = (bf16[128,1536]{1,0:T(8,128)(2,1)}, bf16[128,1536]{1,0:T(8,128)(2,1)S(1)}, u32[]{:S(2)}, u32[]{:S(2)}) collective-permute-start(bf16[128,1536]{1,0:T(8,128)(2,1)} %param.9), channel_id=1, source_target_pairs={{0,7},{1,0},{2,1},{3,2},{4,3},{5,4},{6,5},{7,6},{8,15},{9,8},{10,9... | collective-permute-start | bytes 1179656 | tf_op jit(solution)/shard_map/ppermute | solution.py:15
  26.7 0.7 copy-start.8
  27.5 320.7 %all-gather.33.cloned.1.call-start = ((), (), s32[]{:S(2)}) async-start(), calls=%async_computation.6 | async-start | bytes 6684672 | tf_op jit(solution)/shard_map/all_gather | solution.py:90
  28.1 373.4 %all-gather.35.cloned.1.call-start = ((), (), s32[]{:S(2)}) async-start(), calls=%async_computation.7 | async-start | bytes 6684672 | tf_op jit(solution)/shard_map/all_gather | solution.py:92
  28.1 8.7 %collective-permute-start.4 = (bf16[128,1536]{1,0:T(8,128)(2,1)}, bf16[128,1536]{1,0:T(8,128)(2,1)S(1)}, u32[]{:S(2)}, u32[]{:S(2)}) collective-permute-start(bf16[128,1536]{1,0:T(8,128)(2,1)} %param.11), channel_id=1, source_target_pairs={{0,1},{1,2},{2,3},{3,4},{4,5},{5,6},{6,7},{7,0},{8,9},{9,10},{10,1... | collective-permute-start | bytes 1179656 | tf_op jit(solution)/shard_map/ppermute | solution.py:15
  36.8 0.7 copy-start.7
  37.6 448.9 %all-gather.29.cloned.1.call-start = ((), (), s32[]{:S(2)}) async-start(), calls=%async_computation.4 | async-start | bytes 6684672 | tf_op jit(solution)/shard_map/all_gather | solution.py:89
  42.4 104.8 %all-to-all-start = ((bf16[16,128,1536]{2,1,0:T(8,128)(2,1)}), bf16[16,128,1536]{2,1,0:T(8,128)(2,1)}, u32[]{:S(2)}, u32[]{:S(2)}) async-start(bf16[16,128,1536]{2,1,0:T(8,128)(2,1)} %concatenate.21), calls=%async_computation | async-start | bytes 12582912 | tf_op jit(solution)/shard_map/all_to_all | solution.py:10
  49.5 479.0 %all-gather.31.cloned.1.call-start = ((), (), s32[]{:S(2)}) async-start(), calls=%async_computation.5 | async-start | bytes 6684672 | tf_op jit(solution)/shard_map/all_gather | solution.py:91
  49.6 8.4 %collective-permute-start.2 = (bf16[128,1536]{1,0:T(8,128)(2,1)S(1)}, bf16[128,1536]{1,0:T(8,128)(2,1)S(1)}, u32[]{:S(2)}, u32[]{:S(2)}) collective-permute-start(bf16[128,1536]{1,0:T(8,128)(2,1)S(1)} %copy-done.5), channel_id=1, source_target_pairs={{0,1},{1,2},{2,3},{3,4},{4,5},{5,6},{6,7},{7,0},{8,9},{9,10},{10,1... | collective-permute-start | bytes 1179656 | tf_op jit(solution)/shard_map/ppermute | solution.py:15
  58.0 0.7 copy-start.9
  330.4 263.4 %collective-permute-start.3 = (f32[12,128]{1,0:T(8,128)S(1)}, f32[12,128]{1,0:T(8,128)S(1)}, u32[]{:S(2)}, u32[]{:S(2)}) collective-permute-start(f32[12,128]{1,0:T(8,128)S(1)} %log_add_fusion), channel_id=1, source_target_pairs={{0,1},{1,2},{2,3},{3,4},{4,5},{5,6},{6,7},{7,0},{8,9},{9,10},{10,1... | collective-permute-start | bytes 18440 | tf_op jit(solution)/shard_map/ppermute | solution.py:15
  346.5 269.0 %collective-permute-start.5 = (f32[12,128]{1,0:T(8,128)S(1)}, f32[12,128]{1,0:T(8,128)S(1)}, u32[]{:S(2)}, u32[]{:S(2)}) collective-permute-start(f32[12,128]{1,0:T(8,128)S(1)} %bitcast.139), channel_id=1, source_target_pairs={{0,1},{1,2},{2,3},{3,4},{4,5},{5,6},{6,7},{7,0},{8,9},{9,10},{10,1... | collective-permute-start | bytes 18440 | tf_op jit(solution)/shard_map/ppermute | solution.py:15
  674.7 12.6 %copy-start.1 = (f32[1000,12]{0,1:T(8,128)S(1)}, f32[1000,12]{0,1:T(8,128)}, u32[]{:S(2)}) copy-start(f32[1000,12]{0,1:T(8,128)} %param.15) | copy-start | bytes 144004
Sparse Core Ops, SparseCore 0:
  17.4 121.3 all-gather.22
  141.0 70.5 all-gather.24
  214.3 60.8 all-gather.26
  277.1 60.8 all-gather.32
  340.6 60.8 all-gather.34
  403.4 61.4 all-gather.28
  467.6 60.8 all-gather.30
